TPU v7x, 256 devices: a whole 4x4x8 slice. The times are simulated.
256 devices in a mesh: section: 16 (over z_lo, y), dp: 16 (over x, z_hi, core).
Axes of the slice: x: 4, y: 4, z: 8 (z_hi: 2, z_lo: 4; z = z_hi * 4 + z_lo), core: 2. Of those that a mesh axis runs over, the one named last changes fastest.
Arguments:
- enc_state: bfloat16 [16, 512, 4096], P('section', 'dp'), may hold values from -1000 to 1000
- final_gain: float32 [4096], replicated, may hold values from 0.5 to 1.5
- queries: bfloat16 [16, 2048, 4096], P('section', 'dp'), may hold values from -60 to 60
- w_key: bfloat16 [16, 4096, 4096], P('section', None, 'dp'), may hold values from -0.09375 to 0.09375
- w_value: bfloat16 [16, 4096, 4096], P('section', None, 'dp'), may hold values from -0.09375 to 0.09375
- ctx_grad: bfloat16 [16, 2048, 4096], P('section', 'dp'), may hold values from -6 to 6
- mem_len: int32 [16], P('dp'), may hold values from 8 to 32, as said below
Outputs:
- query_grad: bfloat16 [16, 2048, 4096], P('section', 'dp')
- key_weight_grad: bfloat16 [16, 4096, 4096], P('section', None, 'dp')
- value_weight_grad: bfloat16 [16, 4096, 4096], P('section', None, 'dp')
- state_grad: bfloat16 [16, 512, 4096], P('section', 'dp')
- gain_grad: float32 [4096], replicated
Inputs may be any that keep to these rules, and one draw needn't show every extreme that they name: Sequence b's memory holds mem_len[b] valid tokens from position 0; in every draw some sequence has all 32.
All inputs are finite; a program needn't handle non-finite values.
Results may differ from a plain program's by a relative error of at most 0.028.
The roundings to bfloat16 on the way count: a program that leaves them out, or rounds other values in their place, can miss the bound.
Values may be sent and summed in bfloat16 or wider, within the bound.
A program may use at most 64 MiB of HBM per device.

v0:
```python
import jax
import jax.numpy as jnp
from jax import lax
from jax.sharding import PartitionSpec as P

HEAD_DIM = 256
epsilon = 1e-06


def broadcast(block, axis, holder):
    block = jnp.where(lax.axis_index(axis) == holder, block, jnp.zeros_like(block))
    return lax.psum(block, axis)


def on_device(enc_state, final_gain, queries, w_key, w_value, ctx_grad, mem_len):
    sections = lax.axis_size("section")
    replicas = lax.axis_size("dp")
    section_index = lax.axis_index("section")
    last_encoder = sections // 2 - 1
    is_decoder = (section_index > last_encoder).astype(jnp.float32)
    is_last = (section_index == last_encoder).astype(jnp.float32)
    src_len = enc_state.shape[1]
    tgt_len = queries.shape[1]
    local_width = w_key.shape[2]
    heads_here = local_width // HEAD_DIM
    score_scale = HEAD_DIM ** (-0.5)
    enc_rows = enc_state[0].astype(jnp.float32)
    inverse = lax.rsqrt(jnp.mean(enc_rows * enc_rows, axis=1, keepdims=True) + epsilon)
    normed = enc_rows * inverse
    memory = (normed * final_gain).astype(jnp.bfloat16)
    sent = broadcast(memory, "section", last_encoder)
    all_memory, all_len = (
        lax.all_gather(sent, "dp", axis=0, tiled=True),
        lax.all_gather(mem_len, "dp", axis=0, tiled=True),
    )
    w_both = jnp.concatenate([w_key[0], w_value[0]], axis=1)
    projected = jnp.dot(all_memory, w_both, preferred_element_type=jnp.float32).astype(jnp.bfloat16)
    key_rows = projected[:, :local_width].reshape(replicas, src_len, heads_here, HEAD_DIM)
    value_rows = projected[:, local_width:].reshape(replicas, src_len, heads_here, HEAD_DIM)
    query_heads, grad_heads = (
        lax.all_to_all(queries[0], "dp", split_axis=1, concat_axis=0, tiled=True),
        lax.all_to_all(ctx_grad[0], "dp", split_axis=1, concat_axis=0, tiled=True),
    )
    query_rows = query_heads.reshape(replicas, tgt_len, heads_here, HEAD_DIM)
    grad_rows = grad_heads.reshape(replicas, tgt_len, heads_here, HEAD_DIM)
    key_valid = jnp.arange(src_len, dtype=jnp.int32)[None, :] < all_len[:, None]
    scores = (
        jnp.einsum("btha,buha->bhut", query_rows, key_rows, preferred_element_type=jnp.float32)
        * score_scale
    )
    scores = jnp.where(key_valid[:, None, :, None], scores, -1e30)
    row_max = jnp.max(scores, axis=2, keepdims=True)
    exponent = jnp.exp(scores - row_max)
    probs = exponent / jnp.sum(exponent, axis=2, keepdims=True)
    probs_low = probs.astype(jnp.bfloat16)
    grad_probs = jnp.einsum(
        "btha,buha->bhut", grad_rows, value_rows, preferred_element_type=jnp.float32
    )
    row_delta = jnp.sum(probs * grad_probs, axis=2, keepdims=True)
    grad_scores = (probs * (grad_probs - row_delta) * score_scale).astype(jnp.bfloat16)
    query_grad_heads = (
        jnp.einsum("bhut,buha->btha", grad_scores, key_rows, preferred_element_type=jnp.float32)
        .astype(jnp.bfloat16)
        .reshape(replicas * tgt_len, local_width)
    )
    key_grad = (
        jnp.einsum("bhut,btha->buha", grad_scores, query_rows, preferred_element_type=jnp.float32)
        .astype(jnp.bfloat16)
        .reshape(replicas * src_len, local_width)
    )
    value_grad = (
        jnp.einsum("bhut,btha->buha", probs_low, grad_rows, preferred_element_type=jnp.float32)
        .astype(jnp.bfloat16)
        .reshape(replicas * src_len, local_width)
    )
    both_grads = jnp.concatenate([key_grad, value_grad], axis=1)
    weight_grads = (
        lax.dot_general(
            all_memory, both_grads, (((0,), (0,)), ((), ())), preferred_element_type=jnp.float32
        )
        * is_decoder
    ).astype(jnp.bfloat16)
    query_back = lax.all_to_all(query_grad_heads, "dp", split_axis=0, concat_axis=1, tiled=True)
    query_grad = (query_back.astype(jnp.float32) * is_decoder).astype(jnp.bfloat16)[None]
    section_part = lax.psum_scatter(
        (
            lax.dot_general(
                both_grads, w_both, (((1,), (1,)), ((), ())), preferred_element_type=jnp.float32
            )
            * is_decoder
        ).astype(jnp.bfloat16),
        "dp",
        scatter_dimension=0,
        tiled=True,
    )
    memory_grad = lax.psum(section_part, "section").astype(jnp.float32)
    scaled_grad = memory_grad * final_gain
    last_grad = inverse * (
        scaled_grad - normed * jnp.mean(scaled_grad * normed, axis=1, keepdims=True)
    )
    state_grad = (last_grad * is_last).astype(jnp.bfloat16)[None]
    gain_grad = lax.psum(jnp.sum(memory_grad * normed, axis=0) * is_last, ("section", "dp"))
    key_weight_grad = weight_grads[:, :local_width][None]
    value_weight_grad = weight_grads[:, local_width:][None]
    return (query_grad, key_weight_grad, value_weight_grad, state_grad, gain_grad)


def solution(mesh):
    placed = (
        P("section", "dp", None),
        P(),
        P("section", "dp", None),
        P("section", None, "dp"),
        P("section", None, "dp"),
        P("section", "dp", None),
        P("dp"),
    )
    return jax.shard_map(
        on_device,
        mesh=mesh,
        in_specs=placed,
        out_specs=(
            P("section", "dp", None),
            P("section", None, "dp"),
            P("section", None, "dp"),
            P("section", "dp", None),
            P(),
        ),
        check_vma=False,
    )
```

profile of v0, /device:TPU:1, one launch (start us, length us, event | category | flops | bytes accessed | tf_op | source)
XLA Modules:
  0.0 639.9 jit_solution(12333519288310503521)
XLA Ops:
  7.2 1.2 fusion.28
  8.4 1.8 fusion.33
  10.3 156.1 %all-reduce.4.cloned.1.call-done = bf16[32,4096]{1,0:T(8,128)(2,1)} async-done(((bf16[32,4096]{1,0:T(8,128)(2,1)}), bf16[32,4096]{1,0:T(8,128)(2,1)}) %all-reduce.4.cloned.1.call-update) | async-done | bytes 262160 | tf_op jit(solution)/shard_map/psum | solution.py:12
  166.4 1.6 copy.13
  168.0 1.3 copy.14
  169.3 19.1 %all-to-all-start = ((bf16[128,16,256]{2,0,1:T(8,128)(2,1)}), bf16[128,16,256]{2,0,1:T(8,128)(2,1)S(1)}, u32[]{:S(2)}, u32[]{:S(2)}) async-start(bf16[128,16,256]{2,0,1:T(8,128)(2,1)} %copy.14), calls=%async_computation | async-start | bytes 2097152 | tf_op jit(solution)/shard_map/all_to_all | solution.py:41
  189.1 1.3 copy.16
  190.4 26.1 %all-to-all-done = bf16[128,16,256]{2,0,1:T(8,128)(2,1)S(1)} async-done(((bf16[128,16,256]{2,0,1:T(8,128)(2,1)}), bf16[128,16,256]{2,0,1:T(8,128)(2,1)S(1)}, u32[]{:S(2)}, u32[]{:S(2)}) %all-to-all-start) | async-done | bytes 1048608 | tf_op jit(solution)/shard_map/all_to_all | solution.py:41
  216.5 7.5 %all-to-all-start.1 = ((bf16[128,16,256]{2,0,1:T(8,128)(2,1)}), bf16[128,16,256]{2,0,1:T(8,128)(2,1)S(1)}, u32[]{:S(2)}, u32[]{:S(2)}) async-start(bf16[128,16,256]{2,0,1:T(8,128)(2,1)} %copy.16), calls=%async_computation.1 | async-start | bytes 2097152 | tf_op jit(solution)/shard_map/all_to_all | solution.py:42
  225.3 0.8 dynamic-update-slice
  226.0 33.3 %all-reduce = s32[16]{0:T(128)S(1)} all-reduce(s32[16]{0:T(128)S(1)} %dynamic-update-slice), channel_id=1, replica_groups=mesh['section'=16,'dp'=16] {'dp'}, use_global_device_ids=true, to_apply=%add | all-reduce | flops 16 | bytes 128
  259.4 15.6 %all-gather.2.cloned.1.call-done = bf16[512,4096]{1,0:T(8,128)(2,1)} async-done(((bf16[32,4096]{1,0:T(8,128)(2,1)}), bf16[512,4096]{1,0:T(8,128)(2,1)}) %all-gather.2.cloned.1.call-update) | async-done | bytes 4194320 | tf_op jit(solution)/shard_map/all_gather | solution.py:33
  275.0 5.8 fusion.4
  283.0 6.6 %multiply_convert_fusion = bf16[512,4096]{1,0:T(8,128)(2,1)} fusion(f32[]{:T(128)S(6)} %convert_element_type.108, bf16[4096,256]{1,0:T(8,128)(2,1)} %bitcast.67, bf16[4096,256]{1,0:T(8,128)(2,1)} %bitcast.69, bf16[512,256]{1,0:T(8,128)(2,1)S(1)} %bitcast.70, bf16[512,256]{1,0:T(8,128)(2,1)S(1)} %bitcast.72), kind=kOutput, calls=%fused_computation.2 | convolution fusion | flops 2161115136 | bytes 8912900 | tf_op jit(solution)/shard_map/dot_general | solution.py:87
  289.6 1.5 fusion.3
  291.1 3.7 all-to-all-start.2
  294.8 4.6 multiply_convert_fusion.1
  299.4 2.3 slice_bitcast_fusion
  301.7 91.4 %reduce-scatter.2.cloned.1.call-done = bf16[32,4096]{1,0:T(8,128)(2,1)} async-done(((bf16[512,4096]{1,0:T(8,128)(2,1)}), bf16[32,4096]{1,0:T(8,128)(2,1)}) %reduce-scatter.2.cloned.1.call-update) | async-done | bytes 262160 | tf_op jit(solution)/shard_map/reduce_scatter | solution.py:85
  393.5 1.3 copy.17
  394.8 150.1 %all-reduce.6.cloned.1.call-done = bf16[32,4096]{1,0:T(8,128)(2,1)} async-done(((bf16[32,4096]{1,0:T(8,128)(2,1)}), bf16[32,4096]{1,0:T(8,128)(2,1)}) %all-reduce.6.cloned.1.call-update) | async-done | bytes 262160 | tf_op jit(solution)/shard_map/psum | solution.py:96
  544.9 1.3 fusion.27
  546.2 85.3 %psum.23 = f32[4096]{0:T(1024)} all-reduce(f32[4096]{0:T(1024)S(1)} %broadcast_multiply_fusion), channel_id=1, replica_groups=mesh['section'=16,'dp'=16] {'section','dp'}, use_global_device_ids=true, to_apply=%region_9.10 | all-reduce | flops 4096 | bytes 32768 | tf_op jit(solution)/shard_map/psum | solution.py:102
  631.5 1.8 fusion.34
  (32 shorter events, 4.0 us)
Async XLA Ops:
  7.2 181.2 %copy-start.1 = (bf16[1,128,4096]{2,1,0:T(8,128)(2,1)S(1)}, bf16[1,128,4096]{2,1,0:T(8,128)(2,1)}, u32[]{:S(2)}) copy-start(bf16[1,128,4096]{2,1,0:T(8,128)(2,1)} %param.12) | copy-start | bytes 3145732
  7.2 159.2 %all-reduce.4.cloned.1.call-start = ((), (), s32[]{:S(2)}) async-start(), calls=%async_computation.4 | async-start | bytes 524288 | tf_op jit(solution)/shard_map/psum | solution.py:12
  10.3 264.7 %all-gather.2.cloned.1.call-start = ((), (), s32[]{:S(2)}) async-start(), calls=%async_computation.5 | async-start | bytes 4456448 | tf_op jit(solution)/shard_map/all_gather | solution.py:33
  169.3 55.3 %copy-start.3 = (u32[256]{0:T(256)S(1)}, u32[256]{0:T(256)}, u32[]{:S(2)}) copy-start(u32[256]{0:T(256)} %constant.31) | copy-start | bytes 3076
  169.3 47.2 %all-to-all-start = ((bf16[128,16,256]{2,0,1:T(8,128)(2,1)}), bf16[128,16,256]{2,0,1:T(8,128)(2,1)S(1)}, u32[]{:S(2)}, u32[]{:S(2)}) async-start(bf16[128,16,256]{2,0,1:T(8,128)(2,1)} %copy.14), calls=%async_computation | async-start | bytes 2097152 | tf_op jit(solution)/shard_map/all_to_all | solution.py:41
  216.5 65.4 %all-to-all-start.1 = ((bf16[128,16,256]{2,0,1:T(8,128)(2,1)}), bf16[128,16,256]{2,0,1:T(8,128)(2,1)S(1)}, u32[]{:S(2)}, u32[]{:S(2)}) async-start(bf16[128,16,256]{2,0,1:T(8,128)(2,1)} %copy.16), calls=%async_computation.1 | async-start | bytes 2097152 | tf_op jit(solution)/shard_map/all_to_all | solution.py:42
  224.0 169.2 %reduce-scatter.2.cloned.1.call-start = ((), (), s32[]{:S(2)}) async-start(), calls=%async_computation.6 | async-start | bytes 4456448 | tf_op jit(solution)/shard_map/reduce_scatter | solution.py:85
  291.1 102.1 %all-to-all-start.2 = ((bf16[16,128,256]{1,2,0:T(8,128)(2,1)}), bf16[16,128,256]{1,2,0:T(8,128)(2,1)S(1)}, u32[]{:S(2)}, u32[]{:S(2)}) async-start(bf16[16,128,256]{1,2,0:T(8,128)(2,1)} %fusion.3), calls=%async_computation.2 | async-start | bytes 2097152 | tf_op jit(solution)/shard_map/all_to_all | solution.py:83
  294.8 250.1 %all-reduce.6.cloned.1.call-start = ((), (), s32[]{:S(2)}) async-start(), calls=%async_computation.7 | async-start | bytes 524288 | tf_op jit(solution)/shard_map/psum | solution.py:96
  301.7 243.2 %copy-start = (bf16[1,32,4096]{2,1,0:T(8,128)(2,1)S(1)}, bf16[1,32,4096]{2,1,0:T(8,128)(2,1)}, u32[]{:S(2)}) copy-start(bf16[1,32,4096]{2,1,0:T(8,128)(2,1)} %param.7) | copy-start | bytes 786436
  301.7 243.2 %copy-start.2 = (f32[4096]{0:T(1024)S(1)}, f32[4096]{0:T(1024)}, u32[]{:S(2)}) copy-start(f32[4096]{0:T(1024)} %param.8) | copy-start | bytes 49156
Sparse Core Ops, SparseCore 0:
  11.2 155.1 all-reduce.3
  169.1 105.8 all-gather.1
  289.7 103.3 reduce-scatter.1
  395.6 149.2 all-reduce.5
where the time goes:
time: 640 us
  waiting for transfers between devices  439 us (69%)
  blocking collectives  119 us (19%)
  starting transfers between devices  30.4 us (5%)
  matrix products  19.9 us (3%)
  between operations  14.6 us (2%)
  local copies, waits for them, and re-layouts  9.89 us (2%)
  other arithmetic  7.1 us (1%)
    psum x1, waiting for transfers between devices, broadcast(): return lax.psum(block, axis)  156 us
    psum x1, waiting for transfers between devices, on_device(): memory_grad = lax.psum(section_part, 'section').astype(jnp.float32)  150 us
    reduce_scatter x1, waiting for transfers between devices, on_device(): lax.psum_scatter((lax.dot_general(both_grads, w_both, (((1,), (1,)), ((),...  91.4 us
    psum x1, blocking collectives, on_device(): lax.psum(jnp.sum(memory_grad * normed, axis=0) * is_last, ('section', 'dp'))  85.3 us
    unnamed x1, blocking collectives  33.3 us
    all_to_all x1, waiting for transfers between devices, on_device(): lax.all_to_all(queries[0], 'dp', split_axis=1, concat_axis=0, tiled=True)  26.1 us
    all_to_all x1, starting transfers between devices, on_device(): lax.all_to_all(queries[0], 'dp', split_axis=1, concat_axis=0, tiled=True)  19.1 us
    all_gather x1, waiting for transfers between devices, on_device(): lax.all_gather(sent, 'dp', axis=0, tiled=True)  15.6 us
  transfers between devices with their start and end apart: 7, of which 5 were waited for; matrix products, arithmetic and copies ran while one was open for 4% of the time, Pallas kernels for 0%

commit v1 on v0

--- a/solution.py
+++ b/solution.py
@@ -9,7 +9,7 @@
 
 def broadcast(block, axis, holder):
     block = jnp.where(lax.axis_index(axis) == holder, block, jnp.zeros_like(block))
-    return lax.psum(block, axis)
+    return jnp.sum(lax.all_gather(block, axis), axis=0)
 
 
 def on_device(enc_state, final_gain, queries, w_key, w_value, ctx_grad, mem_len):

time: 640 us -> 568 us (0.89)
  waiting for transfers between devices: 439 us -> 356 us
  blocking collectives: 119 us -> 128 us
    psum x1 -> x0, waiting for transfers between devices: 156 us -> none  [broadcast(): return lax.psum(block, axis)]
    all_gather x0 -> x1, waiting for transfers between devices: none -> 82 us  [broadcast(): return jnp.sum(lax.all_gather(block, axis), axis=0)]
    all_gather x1, waiting for transfers between devices: 15.6 us -> 6.01 us  [on_device(): lax.all_gather(sent, 'dp', axis=0, tiled=True)]
    unnamed x1, blocking collectives: 33.3 us -> 42.7 us
where the time goes in v1:
time: 568 us
  waiting for transfers between devices  356 us (63%)
  blocking collectives  128 us (23%)
  starting transfers between devices  29.2 us (5%)
  matrix products  20 us (4%)
  between operations  14.6 us (3%)
  other arithmetic  10.8 us (2%)
  local copies, waits for them, and re-layouts  8.94 us (2%)
    psum x1, waiting for transfers between devices, on_device(): memory_grad = lax.psum(section_part, 'section').astype(jnp.float32)  150 us
    reduce_scatter x1, waiting for transfers between devices, on_device(): lax.psum_scatter((lax.dot_general(both_grads, w_both, (((1,), (1,)), ((),...  90.5 us
    psum x1, blocking collectives, on_device(): lax.psum(jnp.sum(memory_grad * normed, axis=0) * is_last, ('section', 'dp'))  85.3 us
    all_gather x1, waiting for transfers between devices, broadcast(): return jnp.sum(lax.all_gather(block, axis), axis=0)  82 us
    unnamed x1, blocking collectives  42.7 us
    all_to_all x1, waiting for transfers between devices, on_device(): lax.all_to_all(queries[0], 'dp', split_axis=1, concat_axis=0, tiled=True)  27.3 us
    all_to_all x1, starting transfers between devices, on_device(): lax.all_to_all(queries[0], 'dp', split_axis=1, concat_axis=0, tiled=True)  17.7 us
  transfers between devices with their start and end apart: 7, of which 5 were waited for; matrix products, arithmetic and copies ran while one was open for 4% of the time, Pallas kernels for 0%

profile of v1, /device:TPU:1, one launch (start us, length us, event | category | flops | bytes accessed | tf_op | source)
XLA Modules:
  0.0 567.5 jit_solution(3290258193073889402)
XLA Ops:
  7.2 1.2 fusion.26
  8.4 1.8 fusion.34
  10.3 82.0 %all-gather.3.cloned.1.call-done = bf16[16,32,4096]{2,1,0:T(8,128)(2,1)} async-done(((bf16[1,32,4096]{2,1,0:T(8,128)(2,1)}), bf16[16,32,4096]{2,1,0:T(8,128)(2,1)}) %all-gather.3.cloned.1.call-update) | async-done | bytes 4194320 | tf_op jit(solution)/shard_map/all_gather | solution.py:12
  92.3 3.7 reduce_sum.58
  96.7 1.3 copy.19
  98.1 17.7 %all-to-all-start = ((bf16[128,16,256]{2,0,1:T(8,128)(2,1)}), bf16[128,16,256]{2,0,1:T(8,128)(2,1)S(1)}, u32[]{:S(2)}, u32[]{:S(2)}) async-start(bf16[128,16,256]{2,0,1:T(8,128)(2,1)} %copy.19), calls=%async_computation | async-start | bytes 2097152 | tf_op jit(solution)/shard_map/all_to_all | solution.py:41
  116.4 1.3 copy.21
  117.7 27.3 %all-to-all-done = bf16[128,16,256]{2,0,1:T(8,128)(2,1)S(1)} async-done(((bf16[128,16,256]{2,0,1:T(8,128)(2,1)}), bf16[128,16,256]{2,0,1:T(8,128)(2,1)S(1)}, u32[]{:S(2)}, u32[]{:S(2)}) %all-to-all-start) | async-done | bytes 1048608 | tf_op jit(solution)/shard_map/all_to_all | solution.py:41
  145.0 7.5 %all-to-all-start.1 = ((bf16[128,16,256]{2,0,1:T(8,128)(2,1)}), bf16[128,16,256]{2,0,1:T(8,128)(2,1)S(1)}, u32[]{:S(2)}, u32[]{:S(2)}) async-start(bf16[128,16,256]{2,0,1:T(8,128)(2,1)} %copy.21), calls=%async_computation.1 | async-start | bytes 2097152 | tf_op jit(solution)/shard_map/all_to_all | solution.py:42
  153.8 0.8 dynamic-update-slice
  154.5 42.7 %all-reduce = s32[16]{0:T(128)S(1)} all-reduce(s32[16]{0:T(128)S(1)} %dynamic-update-slice), channel_id=1, replica_groups=mesh['section'=16,'dp'=16] {'dp'}, use_global_device_ids=true, to_apply=%add | all-reduce | flops 16 | bytes 128
  197.3 6.0 %all-gather.5.cloned.1.call-done = bf16[512,4096]{1,0:T(8,128)(2,1)} async-done(((bf16[32,4096]{1,0:T(8,128)(2,1)}), bf16[512,4096]{1,0:T(8,128)(2,1)}) %all-gather.5.cloned.1.call-update) | async-done | bytes 4194320 | tf_op jit(solution)/shard_map/all_gather | solution.py:33
  203.4 5.8 %fusion.4 = bf16[512,512]{1,0:T(8,128)(2,1)S(1)} fusion(bf16[512,4096]{1,0:T(8,128)(2,1)} %all-gather.5.cloned.1.call-done, bf16[4096,256]{1,0:T(8,128)(2,1)} %bitcast.81, bf16[4096,256]{1,0:T(8,128)(2,1)} %bitcast.83), kind=kOutput, calls=%fused_computation.11 | convolution fusion | flops 2156134400 | bytes 8912896 | tf_op jit(solution)/shard_map/dot_general | solution.py:37
  211.4 6.6 %multiply_convert_fusion = bf16[512,4096]{1,0:T(8,128)(2,1)} fusion(f32[]{:T(128)S(6)} %convert_element_type.115, bf16[4096,256]{1,0:T(8,128)(2,1)} %bitcast.82, bf16[4096,256]{1,0:T(8,128)(2,1)} %bitcast.84, bf16[512,256]{1,0:T(8,128)(2,1)S(1)} %bitcast.85, bf16[512,256]{1,0:T(8,128)(2,1)S(1)} %bitcast.87), kind=kOutput, calls=%fused_computation.2 | convolution fusion | flops 2161115136 | bytes 8912900 | tf_op jit(solution)/shard_map/dot_general | solution.py:87
  218.0 1.5 fusion.3
  219.4 3.7 all-to-all-start.2
  223.4 4.6 multiply_convert_fusion.1
  228.0 2.3 slice_bitcast_fusion
  230.3 90.5 %reduce-scatter.2.cloned.1.call-done = bf16[32,4096]{1,0:T(8,128)(2,1)} async-done(((bf16[512,4096]{1,0:T(8,128)(2,1)}), bf16[32,4096]{1,0:T(8,128)(2,1)}) %reduce-scatter.2.cloned.1.call-update) | async-done | bytes 262160 | tf_op jit(solution)/shard_map/reduce_scatter | solution.py:85
  321.1 1.3 copy.22
  322.4 150.1 %all-reduce.3.cloned.1.call-done = bf16[32,4096]{1,0:T(8,128)(2,1)} async-done(((bf16[32,4096]{1,0:T(8,128)(2,1)}), bf16[32,4096]{1,0:T(8,128)(2,1)}) %all-reduce.3.cloned.1.call-update) | async-done | bytes 262160 | tf_op jit(solution)/shard_map/psum | solution.py:96
  472.5 1.3 fusion.29
  473.8 85.3 %psum.15 = f32[4096]{0:T(1024)} all-reduce(f32[4096]{0:T(1024)S(1)} %broadcast_multiply_fusion), channel_id=1, replica_groups=mesh['section'=16,'dp'=16] {'section','dp'}, use_global_device_ids=true, to_apply=%region_9.10 | all-reduce | flops 4096 | bytes 32768 | tf_op jit(solution)/shard_map/psum | solution.py:102
  559.1 1.8 fusion.35
  (35 shorter events, 4.9 us)
Async XLA Ops:
  7.2 88.9 %copy-start.1 = (bf16[1,128,4096]{2,1,0:T(8,128)(2,1)S(1)}, bf16[1,128,4096]{2,1,0:T(8,128)(2,1)}, u32[]{:S(2)}) copy-start(bf16[1,128,4096]{2,1,0:T(8,128)(2,1)} %param.9) | copy-start | bytes 3145732
  7.2 85.1 %all-gather.3.cloned.1.call-start = ((), (), s32[]{:S(2)}) async-start(), calls=%async_computation.4 | async-start | bytes 4456448 | tf_op jit(solution)/shard_map/all_gather | solution.py:12
  10.3 193.1 %all-gather.5.cloned.1.call-start = ((), (), s32[]{:S(2)}) async-start(), calls=%async_computation.5 | async-start | bytes 4456448 | tf_op jit(solution)/shard_map/all_gather | solution.py:33
  96.0 19.7 %copy-start.2 = (bf16[1,128,4096]{2,1,0:T(8,128)(2,1)S(1)}, bf16[1,128,4096]{2,1,0:T(8,128)(2,1)}, u32[]{:S(2)}) copy-start(bf16[1,128,4096]{2,1,0:T(8,128)(2,1)} %param.12) | copy-start | bytes 3145732
  98.0 55.1 %copy-start.4 = (u32[256]{0:T(256)S(1)}, u32[256]{0:T(256)}, u32[]{:S(2)}) copy-start(u32[256]{0:T(256)} %constant.32) | copy-start | bytes 3076
  98.1 46.9 %all-to-all-start = ((bf16[128,16,256]{2,0,1:T(8,128)(2,1)}), bf16[128,16,256]{2,0,1:T(8,128)(2,1)S(1)}, u32[]{:S(2)}, u32[]{:S(2)}) async-start(bf16[128,16,256]{2,0,1:T(8,128)(2,1)} %copy.19), calls=%async_computation | async-start | bytes 2097152 | tf_op jit(solution)/shard_map/all_to_all | solution.py:41
  145.0 65.3 %all-to-all-start.1 = ((bf16[128,16,256]{2,0,1:T(8,128)(2,1)}), bf16[128,16,256]{2,0,1:T(8,128)(2,1)S(1)}, u32[]{:S(2)}, u32[]{:S(2)}) async-start(bf16[128,16,256]{2,0,1:T(8,128)(2,1)} %copy.21), calls=%async_computation.1 | async-start | bytes 2097152 | tf_op jit(solution)/shard_map/all_to_all | solution.py:42
  152.5 168.3 %reduce-scatter.2.cloned.1.call-start = ((), (), s32[]{:S(2)}) async-start(), calls=%async_computation.6 | async-start | bytes 4456448 | tf_op jit(solution)/shard_map/reduce_scatter | solution.py:85
  219.4 101.3 %all-to-all-start.2 = ((bf16[16,128,256]{1,2,0:T(8,128)(2,1)}), bf16[16,128,256]{1,2,0:T(8,128)(2,1)S(1)}, u32[]{:S(2)}, u32[]{:S(2)}) async-start(bf16[16,128,256]{1,2,0:T(8,128)(2,1)} %fusion.3), calls=%async_computation.2 | async-start | bytes 2097152 | tf_op jit(solution)/shard_map/all_to_all | solution.py:83
  223.2 249.3 %all-reduce.3.cloned.1.call-start = ((), (), s32[]{:S(2)}) async-start(), calls=%async_computation.7 | async-start | bytes 524288 | tf_op jit(solution)/shard_map/psum | solution.py:96
  230.3 242.2 %copy-start = (bf16[1,32,4096]{2,1,0:T(8,128)(2,1)S(1)}, bf16[1,32,4096]{2,1,0:T(8,128)(2,1)}, u32[]{:S(2)}) copy-start(bf16[1,32,4096]{2,1,0:T(8,128)(2,1)} %param.7) | copy-start | bytes 786436
  230.3 242.2 %copy-start.3 = (f32[4096]{0:T(1024)S(1)}, f32[4096]{0:T(1024)}, u32[]{:S(2)}) copy-start(f32[4096]{0:T(1024)} %param.8) | copy-start | bytes 49156
Sparse Core Ops, SparseCore 0:
  10.4 81.8 all-gather.2
  96.2 107.1 all-gather.4
  218.1 102.5 reduce-scatter.1
  323.2 149.2 all-reduce.2
